TPU v7x, 32 devices: a whole 2x2x4 slice. The times are simulated.
32 devices in a mesh: row: 4 (over z), col: 8 (over y, x, core).
Axes of the slice: x: 2, y: 2, z: 4, core: 2. Of those that a mesh axis runs over, the one named last changes fastest.
Arguments:
- inv_depth: float32 [64, 3072], P(('row', 'col')), may hold values from 0.2 to 1
- rotation: float32 [3, 64], P(None, ('row', 'col')), may hold values from -0.05 to 0.05
- translation: float32 [3, 64], P(None, ('row', 'col')), may hold values from -0.25 to 0.25
- edge_target: int32 [64, 24], P(('row', 'col')), may hold values from 0 to 63, as said below
- flow_obs: float32 [2, 64, 24, 3072], P(None, ('row', 'col')), may hold values from -2.8 to 2.8
- weight: float32 [2, 64, 24, 3072], P(None, ('row', 'col')), may hold values from 0.1 to 1
Outputs:
- depth_next: float32 [64, 3072], P(('row', 'col'))
- pose_step: float32 [6, 64], P(None, ('row', 'col'))
Inputs may be any that keep to these rules, and one draw needn't show every extreme that they name: `edge_target`: each keyframe's targets are distinct, differ from the keyframe itself, are sorted ascending, and lie in the keyframe's own block of 16 consecutive keyframes or in one of the two neighbouring blocks, the blocks counted cyclically.
All inputs are finite; a program needn't handle non-finite values.
Results may differ from a plain program's by a relative error of at most 0.0003.
Values sent between devices are 32-bit elements; how exact they have to be, the bound alone decides.
No kernel may reach another device: no remote copies, remote signals or barrier semaphores. Data moves between devices by JAX's collectives and lax.ppermute only.
A program may use at most 128 MiB of HBM per device.

v0:
```python
import jax
import jax.numpy as jnp
from jax import lax
from jax.sharding import PartitionSpec as P

IMG_H = 48
IMG_W = 64
PRECISE = lax.Precision.HIGHEST
DAMP_DEPTH = 0.1
LEVENBERG = 0.1
RIDGE = 0.001


def with_halo(cells, sides, width):
    for axis, dim in sides:
        count = lax.axis_size(axis)
        head = lax.slice_in_dim(cells, 0, width, axis=dim)
        tail = lax.slice_in_dim(cells, cells.shape[dim] - width, cells.shape[dim], axis=dim)
        cells = jnp.concatenate(
            [
                lax.ppermute(tail, axis, [(i, (i + 1) % count) for i in range(count)]),
                cells,
                lax.ppermute(head, axis, [((i + 1) % count, i) for i in range(count)]),
            ],
            axis=dim,
        )
    return cells


def from_behind(shard, axis, by):
    devices = lax.axis_size(axis)
    return lax.ppermute(shard, axis, [(i, (i + by) % devices) for i in range(devices)])


def pixel_grid(pixel_count):
    pixel_index = jnp.arange(pixel_count, dtype=jnp.int32)
    across = (pixel_index % IMG_W).astype(jnp.float32)
    downward = (pixel_index // IMG_W).astype(jnp.float32)
    return ((across + 0.5) / IMG_W - 0.5, (downward + 0.5 - 0.5 * IMG_H) / IMG_W)


def edge_terms(relative, target_depth, flows, weights, across, downward):
    spin_x, spin_y, spin_z, move_x, move_y, move_z = [relative[i][:, None] for i in range(6)]
    point_x = across + spin_y - spin_z * downward + move_x * target_depth
    point_y = downward + spin_z * across - spin_x + move_y * target_depth
    point_z = 1.0 + spin_x * downward - spin_y * across + move_z * target_depth
    recip_z = 1.0 / point_z
    image_u = point_x * recip_z
    image_v = point_y * recip_z
    resid_u = flows[0] - (image_u - across)
    resid_v = flows[1] - (image_v - downward)
    slope_u = recip_z * (move_x - image_u * move_z)
    slope_v = recip_z * (move_y - image_v * move_z)
    depth_recip = target_depth * recip_z
    blank_map = jnp.zeros_like(recip_z)
    jac_u = jnp.stack(
        [
            -image_u * downward * recip_z,
            (1.0 + image_u * across) * recip_z,
            -downward * recip_z,
            depth_recip,
            blank_map,
            -image_u * depth_recip,
        ]
    )
    jac_v = jnp.stack(
        [
            (-1.0 - image_v * downward) * recip_z,
            image_v * across * recip_z,
            across * recip_z,
            blank_map,
            depth_recip,
            -image_v * depth_recip,
        ]
    )
    weight_u = weights[0]
    weight_v = weights[1]
    depth_grad = weight_u * slope_u * resid_u + weight_v * slope_v * resid_v
    depth_curv = weight_u * slope_u * slope_u + weight_v * slope_v * slope_v
    scaled_u = weight_u * jac_u
    scaled_v = weight_v * jac_v
    coupling = scaled_u * slope_u + scaled_v * slope_v
    block = jnp.einsum("aep,bep->eab", scaled_u, jac_u, precision=PRECISE) + jnp.einsum(
        "aep,bep->eab", scaled_v, jac_v, precision=PRECISE
    )
    pose_grad = jnp.einsum("aep,ep->ea", scaled_u, resid_u, precision=PRECISE) + jnp.einsum(
        "aep,ep->ea", scaled_v, resid_v, precision=PRECISE
    )
    return (depth_grad, depth_curv, coupling, block, pose_grad)


def solve_frames(block_table):
    frame_count = block_table.shape[0]
    matrix = block_table[:, :36].reshape(frame_count, 6, 6).transpose(1, 2, 0)
    right_side = block_table[:, 36:].T
    factor = {}
    for i in range(6):
        for j in range(i + 1):
            element = matrix[i, j]
            if i == j:
                element = element * (1.0 + LEVENBERG) + RIDGE
            for k in range(j):
                element = element - factor[i, k] * factor[j, k]
            factor[i, j] = jnp.sqrt(element) if i == j else element / factor[j, j]
    forward = []
    for i in range(6):
        element = right_side[i]
        for k in range(i):
            element = element - factor[i, k] * forward[k]
        forward.append(element / factor[i, i])
    result = [None] * 6
    for i in reversed(range(6)):
        element = forward[i]
        for k in range(i + 1, 6):
            element = element - factor[k, i] * result[k]
        result[i] = element / factor[i, i]
    return jnp.stack(result, 1)


def spread(values):
    nearby = with_halo(values[None], (("row", 0),), 1)
    return lax.all_gather(nearby, "col", axis=1, tiled=True)


def collect(buffer):
    col_part = lax.psum_scatter(buffer, "col", scatter_dimension=1, tiled=True)
    from_next = from_behind(col_part[0], "row", -1)
    from_prev = from_behind(col_part[2], "row", 1)
    return col_part[1] + from_next + from_prev


def shards(inv_depth, rotation, translation, edge_target, flow_obs, weight):
    frames_dev, pixels = inv_depth.shape
    per_frame = edge_target.shape[1]
    edges = frames_dev * per_frame
    columns = lax.axis_size("col")
    loop_size = lax.axis_size("row")
    group_size = frames_dev * columns
    total_frames = group_size * loop_size
    my_row = lax.axis_index("row")
    first_frame = (my_row * columns + lax.axis_index("col")) * frames_dev
    targets = edge_target.reshape(edges)
    sources = first_frame + jnp.arange(edges, dtype=jnp.int32) // per_frame
    offsets = (targets // group_size - my_row + 1 + loop_size) % loop_size
    slot_index = offsets * group_size + targets % group_size
    across, downward = pixel_grid(pixels)
    pose_parts = (
        lax.all_gather(rotation, ("row", "col"), axis=1, tiled=True),
        lax.all_gather(translation, ("row", "col"), axis=1, tiled=True),
    )
    pose_all = jnp.concatenate(pose_parts, 0)
    frame_ids = jnp.arange(total_frames, dtype=jnp.int32)
    src_hot = (sources[:, None] == frame_ids[None, :]).astype(jnp.float32)
    tgt_hot = (targets[:, None] == frame_ids[None, :]).astype(jnp.float32)
    pair_hot = src_hot - tgt_hot
    relative = jnp.dot(pair_hot, pose_all.T, precision=PRECISE).T
    nearby_depth = spread(inv_depth).reshape(3 * group_size, pixels)
    target_depth = jnp.take(nearby_depth, slot_index, axis=0)
    depth_grad, depth_curv, coupling, block, pose_grad = edge_terms(
        relative,
        target_depth,
        flow_obs.reshape(2, edges, pixels),
        weight.reshape(2, edges, pixels),
        across,
        downward,
    )
    slot_hot = (jnp.arange(3 * group_size, dtype=jnp.int32)[:, None] == slot_index[None, :]).astype(
        jnp.float32
    )

    def coalesce(values):
        flat_rows = values.reshape(edges, -1)
        summed = jnp.dot(slot_hot, flat_rows, precision=PRECISE)
        return summed.reshape((3, group_size) + values.shape[1:])

    depth_sums = collect(coalesce(jnp.stack([depth_grad, depth_curv], 1)))
    grad_sum = depth_sums[:, 0]
    inverse = 1.0 / (DAMP_DEPTH + depth_sums[:, 1])
    scaled = grad_sum * inverse
    returned = spread(jnp.stack([inverse, scaled], 1)).reshape(3 * group_size, 2, pixels)
    at_edges = jnp.take(returned, slot_index, axis=0)
    reduced = block - jnp.einsum(
        "aep,bep->eab", coupling * at_edges[:, 0][None], coupling, precision=PRECISE
    )
    reduced_grad = pose_grad - jnp.einsum("aep,ep->ea", coupling, at_edges[:, 1], precision=PRECISE)
    flat_block = reduced.reshape(edges, 36)
    out_rows = jnp.concatenate([flat_block, reduced_grad], 1)
    in_rows = jnp.concatenate([flat_block, -reduced_grad], 1)
    block_table = jnp.dot(src_hot.T, out_rows, precision=PRECISE) + jnp.dot(
        tgt_hot.T, in_rows, precision=PRECISE
    )
    block_table = lax.psum(block_table, ("row", "col"))
    frame_steps = solve_frames(block_table)
    own_step = lax.dynamic_slice_in_dim(frame_steps, first_frame, frames_dev, 0)
    motion = jnp.dot(pair_hot, frame_steps, precision=PRECISE)
    correction = jnp.einsum("aep,ea->ep", coupling, motion, precision=PRECISE)
    fix_sum = collect(coalesce(correction))
    depth_next = inv_depth + (grad_sum - fix_sum) * inverse
    return (depth_next, own_step.T)


def solution(mesh):
    return jax.shard_map(
        shards,
        mesh=mesh,
        in_specs=(
            P(("row", "col"), None),
            P(None, ("row", "col")),
            P(None, ("row", "col")),
            P(("row", "col"), None),
            P(None, ("row", "col"), None, None),
            P(None, ("row", "col"), None, None),
        ),
        out_specs=(P(("row", "col"), None), P(None, ("row", "col"))),
        check_vma=False,
    )
```

profile of v0, /device:TPU:0, one launch (start us, length us, event | category | flops | bytes accessed | tf_op | source)
XLA Modules:
  0.0 454.0 jit_solution(9152022826286836492)
XLA Ops:
  8.0 5.1 %collective-permute-start.1 = (f32[1,2,3072]{2,0,1:T(1,128)S(1)}, f32[1,2,3072]{2,0,1:T(1,128)S(1)}, u32[]{:S(2)}, u32[]{:S(2)}) collective-permute-start(f32[1,2,3072]{2,0,1:T(1,128)S(1)} %broadcast_in_dim.30), channel_id=1, source_target_pairs={{8,0},{16,8},{24,16},{0,24},{9,1},{17,9},{25,17},{1,25},{10,2},{18... | collective-permute-start | bytes 73736 | tf_op jit(solution)/shard_map/ppermute | solution.py:23
  17.0 42.3 %all-gather = f32[32,2,3]{2,1,0:T(2,128)S(1)} all-gather(f32[1,2,3]{2,1,0:T(2,128)} %bitcast.512), channel_id=1, replica_groups=mesh['row'=4,'col'=8] {'row','col'}, dimensions={0}, use_global_device_ids=true | all-gather | bytes 792 | tf_op jit(solution)/shard_map/all_gather | solution.py:148
  59.4 37.0 %all-gather.1 = f32[32,2,3]{2,1,0:T(2,128)S(1)} all-gather(f32[1,2,3]{2,1,0:T(2,128)} %bitcast.513), channel_id=1, replica_groups=mesh['row'=4,'col'=8] {'row','col'}, dimensions={0}, use_global_device_ids=true | all-gather | bytes 792 | tf_op jit(solution)/shard_map/all_gather | solution.py:149
  97.3 1.8 fusion.181
  101.0 10.5 %all_gather.14 = f32[3,16,3072]{2,0,1:T(4,128)S(1)} all-gather(f32[3,2,3072]{2,0,1:T(4,128)S(1)} %pad_maximum_fusion.1), channel_id=1, replica_groups=mesh['row'=4,'col'=8] {'col'}, dimensions={1}, use_global_device_ids=true | all-gather | bytes 663552 | tf_op jit(solution)/shard_map/all_gather | solution.py:122
  112.8 2.0 multiply_dynamic-update-slice_fusion.3
  114.8 1.5 fusion.32
  116.5 1.8 fusion.17
  118.4 1.3 multiply_dynamic-update-slice_fusion.2
  119.7 1.1 multiply_dynamic-update-slice_fusion.1
  121.6 1.1 constant_dynamic-update-slice_fusion.1
  122.7 1.5 multiply_dynamic-update-slice_fusion
  124.2 48.7 %all-reduce.5.cloned.1.call-done = f32[3,16,2,3072]{3,1,2,0:T(8,128)} async-done(((f32[3,16,2,3072]{3,1,2,0:T(8,128)}), f32[3,16,2,3072]{3,1,2,0:T(8,128)}) %all-reduce.5.cloned.1.call-update) | async-done | bytes 1179664
  172.9 1.1 dynamic-slice_bitcast_fusion.1
  174.0 3.3 collective-permute-start.2
  177.3 1.2 multiply_dynamic-update-slice_fusion.6
  179.1 4.3 collective-permute-done.3
  184.5 2.0 collective-permute-start.4
  186.5 1.1 multiply_dynamic-update-slice_fusion.5
  187.6 1.0 collective-permute-done.5
  188.6 1.9 collective-permute-done.4
  191.8 1.1 constant_dynamic-update-slice_fusion
  193.8 1.2 multiply_dynamic-update-slice_fusion.4
  195.0 1.9 bitcast_subtract_fusion.1
  196.9 15.1 %all-gather.4.cloned.1.call-done = f32[3,16,2,3072]{3,2,0,1:T(2,128)} async-done(((f32[3,2,2,3072]{3,2,0,1:T(2,128)}), f32[3,16,2,3072]{3,2,0,1:T(2,128)}) %all-gather.4.cloned.1.call-update) | async-done | bytes 1179664 | tf_op jit(solution)/shard_map/all_gather | solution.py:122
  212.0 1.7 copy.35
  214.6 1.9 gather_fusion.1
  218.5 9.1 %broadcast_multiply_fusion = (f32[6,48,3072]{2,1,0:T(8,128)}, f32[6,48,3072]{2,1,0:T(8,128)S(1)}, f32[6,48,3072]{2,1,0:T(8,128)}, f32[6,48,3072]{2,1,0:T(8,128)}) fusion(f32[48,3072]{1,0:T(8,128)} %bitcast.500, f32[48,3072]{1,0:T(8,128)} %get-tuple-element.58, f32[48,3072]{1,0:T(8,128)} %get-tuple-element.55, ...), kind=kLoop, calls=%fused_computation.20 | loop fusion | flops 5308416 | bytes 24182784 | tf_op jit(solution)/shard_map/mul | solution.py:183
  227.6 12.9 %fusion.2 = f32[48,1,6]{2,1,0:T(1,128)} fusion(f32[6,48,3072]{2,1,0:T(8,128)S(1)} %get-tuple-element.39, f32[48,2,3072]{2,1,0:T(2,128)S(1)} %broadcast_select_fusion), kind=kOutput, calls=%fused_computation.4 | convolution fusion | flops 10616832 | bytes 4129920 | tf_op jit(solution)/shard_map/aep,ep->ea/dot_general | solution.py:185
  241.3 18.1 %fusion.8 = f32[48,6,6]{2,1,0:T(8,128)} fusion(f32[6,48,3072]{2,1,0:T(8,128)} %get-tuple-element.41, f32[6,48,3072]{2,1,0:T(8,128)} %get-tuple-element.60), kind=kOutput, calls=%fused_computation.10 | convolution fusion | flops 63700992 | bytes 7084800 | tf_op jit(solution)/shard_map/aep,bep->eab/dot_general | solution.py:83
  259.4 12.8 %fusion.6 = f32[48,1,6]{2,1,0:T(1,128)} fusion(f32[6,48,3072]{2,1,0:T(8,128)S(1)} %copy-done.1, f32[48,3072,1]{1,0,2:T(8,128)S(1)} %bitcast.502), kind=kOutput, calls=%fused_computation.8 | convolution fusion | flops 10616832 | bytes 4129920 | tf_op jit(solution)/shard_map/aep,ep->ea/dot_general | solution.py:86
  273.0 16.7 %fusion.19 = f32[48,6,6]{2,1,0:T(8,128)S(1)} fusion(f32[48,6,6]{2,1,0:T(8,128)} %fusion.8, f32[6,48,3072]{2,1,0:T(8,128)} %multiply_dynamic-update-slice_fusion.4, f32[6,48,3072]{2,1,0:T(8,128)} %get-tuple-element.40), kind=kOutput, calls=%fused_computation.28 | convolution fusion | flops 63702720 | bytes 7091712 | tf_op jit(solution)/shard_map/aep,bep->eab/dot_general | solution.py:83
  289.7 13.0 %fusion.10 = f32[48,1,6]{2,1,0:T(1,128)} fusion(f32[6,48,3072]{2,1,0:T(8,128)S(1)} %copy-done, f32[48,3072,1]{1,0,2:T(8,128)S(1)} %bitcast.501), kind=kOutput, calls=%fused_computation.12 | convolution fusion | flops 10616832 | bytes 4129920 | tf_op jit(solution)/shard_map/aep,ep->ea/dot_general | solution.py:86
  302.6 14.9 %fusion.24 = f32[48,6,6]{2,1,0:T(8,128)} fusion(f32[48,6,6]{2,1,0:T(8,128)S(1)} %fusion.19, f32[6,48,3072]{2,1,0:T(8,128)S(1)} %get-tuple-element.39, f32[6,48,3072]{2,1,0:T(8,128)S(1)} %copy-done.2), kind=kOutput, calls=%fused_computation.29 | convolution fusion | flops 63702720 | bytes 7091712 | tf_op jit(solution)/shard_map/aep,bep->eab/dot_general | solution.py:182
  317.5 1.6 reshape.5281
  320.0 1.4 copy.50
  322.4 1.6 convolution_add_fusion
  323.9 39.9 %psum.7 = f32[64,42]{0,1:T(8,128)} all-reduce(f32[64,42]{0,1:T(8,128)} %convolution_add_fusion), channel_id=1, replica_groups=mesh['row'=4,'col'=8] {'row','col'}, use_global_device_ids=true, to_apply=%region_1.2 | all-reduce | flops 2688 | bytes 21504 | tf_op jit(solution)/shard_map/psum | solution.py:192
  364.5 1.3 slice.209
  365.8 1.3 reshape.5249
  367.1 1.0 fusion.157
  369.1 1.4 subtract_divide_fusion
  372.1 6.0 %fusion = f32[48,1,3072]{2,1,0:T(1,128)S(1)} fusion(f32[48,6,1]{1,2,0:T(1,128)S(1)} %bitcast.509, f32[6,48,3072]{2,1,0:T(8,128)S(1)} %get-tuple-element.39), kind=kOutput, calls=%fused_computation.2 | convolution fusion | flops 10616832 | bytes 4129920 | tf_op jit(solution)/shard_map/aep,ea->ep/dot_general | solution.py:196
  378.1 1.3 fusion.29
  379.5 56.4 %all-reduce.7.cloned.1.call-done = f32[3,16,3072]{2,1,0:T(8,128)} async-done(((f32[3,16,3072]{2,1,0:T(8,128)}), f32[3,16,3072]{2,1,0:T(8,128)}) %all-reduce.7.cloned.1.call-update) | async-done | bytes 589840
  436.8 3.3 collective-permute-start.6
  441.6 4.1 collective-permute-done.7
  445.7 1.5 fusion.45
  (101 shorter events, 25.0 us)
Async XLA Ops:
  7.2 92.5 %copy-start.21 = (u32[32]{0:T(128)S(1)}, u32[32]{0:T(128)}, u32[]{:S(2)}) copy-start(u32[32]{0:T(128)} %constant.161) | copy-start | bytes 388
  7.2 165.7 %all-reduce.5.cloned.1.call-start = ((), (), s32[]{:S(2)}) async-start(), calls=%async_computation.1 | async-start | bytes 2359296
  8.0 93.0 %collective-permute-start.1 = (f32[1,2,3072]{2,0,1:T(1,128)S(1)}, f32[1,2,3072]{2,0,1:T(1,128)S(1)}, u32[]{:S(2)}, u32[]{:S(2)}) collective-permute-start(f32[1,2,3072]{2,0,1:T(1,128)S(1)} %broadcast_in_dim.30), channel_id=1, source_target_pairs={{8,0},{16,8},{24,16},{0,24},{9,1},{17,9},{25,17},{1,25},{10,2},{18... | collective-permute-start | bytes 73736 | tf_op jit(solution)/shard_map/ppermute | solution.py:23
  13.1 87.8 %collective-permute-start = (f32[1,2,3072]{2,0,1:T(1,128)S(1)}, f32[1,2,3072]{2,0,1:T(1,128)S(1)}, u32[]{:S(2)}, u32[]{:S(2)}) collective-permute-start(f32[1,2,3072]{2,0,1:T(1,128)S(1)} %broadcast_in_dim.30), channel_id=1, source_target_pairs={{0,8},{8,16},{16,24},{24,0},{1,9},{9,17},{17,25},{25,1},{2,10},{10... | collective-permute-start | bytes 73736 | tf_op jit(solution)/shard_map/ppermute | solution.py:21
  13.9 98.0 %copy-start.20 = (s32[48]{0:T(128)}, s32[48]{0:T(128)S(1)}, u32[]{:S(2)}) copy-start(s32[48]{0:T(128)S(1)} %reshape.5243) | copy-start | bytes 580
  15.9 96.1 %copy-start.22 = (s32[48]{0:T(128)}, s32[48]{0:T(128)S(1)}, u32[]{:S(2)}) copy-start(s32[48]{0:T(128)S(1)} %fusion.82) | copy-start | bytes 580
  99.0 15.8 %copy-start.3 = (f32[1,2,24,3072]{3,2,1,0:T(8,128)}, f32[1,2,24,3072]{3,2,1,0:T(8,128)S(1)}, u32[]{:S(2)}) copy-start(f32[1,2,24,3072]{3,2,1,0:T(8,128)S(1)} %get-tuple-element.72) | copy-start | bytes 1769476
  99.0 15.8 %copy-start.4 = (f32[1,2,24,3072]{3,2,1,0:T(8,128)}, f32[1,2,24,3072]{3,2,1,0:T(8,128)S(1)}, u32[]{:S(2)}) copy-start(f32[1,2,24,3072]{3,2,1,0:T(8,128)S(1)} %get-tuple-element.73) | copy-start | bytes 1769476
  112.8 3.6 copy-start.17
  112.8 3.6 copy-start.18
  116.4 2.0 copy-start.7
  116.4 2.0 copy-start.10
  116.4 2.0 copy-start.11
  116.4 2.0 copy-start.12
  116.4 2.0 copy-start.14
  116.4 2.0 copy-start.15
  116.5 6.3 %copy-start.16 = (f32[48]{0:T(128)S(1)}, f32[48]{0:T(128)}, u32[]{:S(2)}) copy-start(f32[48]{0:T(128)} %get-tuple-element.67) | copy-start | bytes 580
  118.3 93.7 %all-gather.4.cloned.1.call-start = ((), (), s32[]{:S(2)}) async-start(), calls=%async_computation | async-start | bytes 1327104 | tf_op jit(solution)/shard_map/all_gather | solution.py:122
  119.7 66.9 %copy-start.13 = (f32[3072]{0:T(1024)S(1)}, f32[3072]{0:T(1024)}, u32[]{:S(2)}) copy-start(f32[3072]{0:T(1024)} %fusion.76) | copy-start | bytes 36868
  174.0 5.1 %collective-permute-start.2 = (f32[2,2,3072]{2,0,1:T(2,128)S(1)}, f32[2,2,3072]{2,0,1:T(2,128)S(1)}, u32[]{:S(2)}, u32[]{:S(2)}) collective-permute-start(f32[2,2,3072]{2,0,1:T(2,128)S(1)} %get-tuple-element.48), channel_id=1, source_target_pairs={{0,24},{8,0},{16,8},{24,16},{1,25},{9,1},{17,9},{25,17},{2,26},{10... | collective-permute-start | bytes 147464 | tf_op jit(solution)/shard_map/ppermute | solution.py:32
  177.3 6.1 %collective-permute-start.3 = (f32[2,2,3072]{2,0,1:T(2,128)S(1)}, f32[2,2,3072]{2,0,1:T(2,128)S(1)}, u32[]{:S(2)}, u32[]{:S(2)}) collective-permute-start(f32[2,2,3072]{2,0,1:T(2,128)S(1)} %get-tuple-element.49), channel_id=1, source_target_pairs={{0,8},{8,16},{16,24},{24,0},{1,9},{9,17},{17,25},{25,1},{2,10},{10... | collective-permute-start | bytes 147464 | tf_op jit(solution)/shard_map/ppermute | solution.py:32
  184.4 4.2 copy-start.8
  184.4 4.2 copy-start.9
  184.5 4.1 collective-permute-start.5
  184.5 5.9 %collective-permute-start.4 = (f32[1,2,2,3072]{3,1,2,0:T(2,128)S(1)}, f32[1,2,2,3072]{3,1,2,0:T(2,128)S(1)}, u32[]{:S(2)}, u32[]{:S(2)}) collective-permute-start(f32[1,2,2,3072]{3,1,2,0:T(2,128)S(1)} %maximum_bitcast_fusion.1), channel_id=1, source_target_pairs={{0,8},{8,16},{16,24},{24,0},{1,9},{9,17},{17,25},{25,1},{2,10},{10... | collective-permute-start | bytes 147464 | tf_op jit(solution)/shard_map/ppermute | solution.py:21
  191.3 244.5 %all-reduce.7.cloned.1.call-start = ((), (), s32[]{:S(2)}) async-start(), calls=%async_computation.2 | async-start | bytes 1179648
  241.3 18.1 %copy-start.1 = (f32[6,48,3072]{2,1,0:T(8,128)S(1)}, f32[6,48,3072]{2,1,0:T(8,128)}, u32[]{:S(2)}) copy-start(f32[6,48,3072]{2,1,0:T(8,128)} %get-tuple-element.41) | copy-start | bytes 10616836
  241.3 18.1 %copy-start.6 = (f32[48,3072]{1,0:T(8,128)S(1)}, f32[48,3072]{1,0:T(8,128)}, u32[]{:S(2)}) copy-start(f32[48,3072]{1,0:T(8,128)} %get-tuple-element.59) | copy-start | bytes 1769476
  273.0 16.7 %copy-start = (f32[6,48,3072]{2,1,0:T(8,128)S(1)}, f32[6,48,3072]{2,1,0:T(8,128)}, u32[]{:S(2)}) copy-start(f32[6,48,3072]{2,1,0:T(8,128)} %get-tuple-element.40) | copy-start | bytes 10616836
  273.0 16.7 %copy-start.5 = (f32[48,3072]{1,0:T(8,128)S(1)}, f32[48,3072]{1,0:T(8,128)}, u32[]{:S(2)}) copy-start(f32[48,3072]{1,0:T(8,128)} %get-tuple-element.54) | copy-start | bytes 1769476
  289.6 13.0 %copy-start.2 = (f32[6,48,3072]{2,1,0:T(8,128)S(1)}, f32[6,48,3072]{2,1,0:T(8,128)}, u32[]{:S(2)}) copy-start(f32[6,48,3072]{2,1,0:T(8,128)} %get-tuple-element.38) | copy-start | bytes 10616836
  317.5 60.6 %copy-start.19 = (s32[48]{0:T(128)S(1)}, s32[48]{0:T(128)}, u32[]{:S(2)}) copy-start(s32[48]{0:T(128)} %get-tuple-element.45) | copy-start | bytes 580
  436.8 4.8 %collective-permute-start.6 = (f32[2,3072]{1,0:T(2,128)S(1)}, f32[2,3072]{1,0:T(2,128)S(1)}, u32[]{:S(2)}, u32[]{:S(2)}) collective-permute-start(f32[2,3072]{1,0:T(2,128)S(1)} %get-tuple-element.62), channel_id=1, source_target_pairs={{0,24},{8,0},{16,8},{24,16},{1,25},{9,1},{17,9},{25,17},{2,26},{10... | collective-permute-start | bytes 73736 | tf_op jit(solution)/shard_map/ppermute | solution.py:32
  440.1 5.6 %collective-permute-start.7 = (f32[2,3072]{1,0:T(2,128)S(1)}, f32[2,3072]{1,0:T(2,128)S(1)}, u32[]{:S(2)}, u32[]{:S(2)}) collective-permute-start(f32[2,3072]{1,0:T(2,128)S(1)} %get-tuple-element.63), channel_id=1, source_target_pairs={{0,8},{8,16},{16,24},{24,0},{1,9},{9,17},{17,25},{25,1},{2,10},{10... | collective-permute-start | bytes 73736 | tf_op jit(solution)/shard_map/ppermute | solution.py:32
Sparse Core Ops, SparseCore 0:
  118.4 54.4 all-reduce.4
  191.4 20.5 all-gather.3
  379.6 56.1 all-reduce.6
where the time goes:
time: 461 us; the launch traced here: 454 us
  waiting for transfers between devices  133 us (29%)
  blocking collectives  130 us (28%)
  matrix products  101 us (22%)
  other arithmetic  33.8 us (7%)
  local copies, waits for them, and re-layouts  27.4 us (6%)
  between operations  15 us (3%)
  starting transfers between devices  14.4 us (3%)
    unnamed x5, waiting for transfers between devices  105 us
    all_gather x1, blocking collectives, shards(): lax.all_gather(rotation, ('row', 'col'), axis=1, tiled=True)  42.3 us
    psum x1, blocking collectives, shards(): block_table = lax.psum(block_table, ('row', 'col'))  39.9 us
    all_gather x1, blocking collectives, shards(): lax.all_gather(translation, ('row', 'col'), axis=1, tiled=True)  37 us
    dot_general x1, matrix products, edge_terms(): jnp.einsum('aep,bep->eab', scaled_v, jac_v, precision=PRECISE)  18.1 us
    dot_general x1, matrix products, edge_terms(): jnp.einsum('aep,bep->eab', scaled_u, jac_u, precision=PRECISE)  16.7 us
    all_gather x1, waiting for transfers between devices, spread(): return lax.all_gather(nearby, 'col', axis=1, tiled=True)  15.1 us
    dot_general x1, matrix products, shards(): jnp.einsum('aep,bep->eab', coupling * at_edges[:, 0][None], coupling, pre...  14.9 us
  transfers between devices with their start and end apart: 11, of which 9 were waited for; matrix products, arithmetic and copies ran while one was open for 5% of the time, Pallas kernels for 0%

commit v1 on v0

--- a/solution.py
+++ b/solution.py
@@ -189,7 +189,7 @@
     block_table = jnp.dot(src_hot.T, out_rows, precision=PRECISE) + jnp.dot(
         tgt_hot.T, in_rows, precision=PRECISE
     )
-    block_table = lax.psum(block_table, ("row", "col"))
+    block_table = lax.psum(lax.psum(block_table, "row"), "col")
     frame_steps = solve_frames(block_table)
     own_step = lax.dynamic_slice_in_dim(frame_steps, first_frame, frames_dev, 0)
     motion = jnp.dot(pair_hot, frame_steps, precision=PRECISE)

time: 461 us -> 461 us (level)
    psum x1 -> x2, blocking collectives: 39.9 us -> 43.7 us  [shards(): block_table = lax.psum(lax.psum(block_table, 'row'), 'col')]
where the time goes in v1:
time: 461 us; the launch traced here: 454 us
  blocking collectives  133 us (29%)
  waiting for transfers between devices  129 us (28%)
  matrix products  101 us (22%)
  other arithmetic  33.7 us (7%)
  local copies, waits for them, and re-layouts  27.4 us (6%)
  between operations  15.1 us (3%)
  starting transfers between devices  14.4 us (3%)
    unnamed x5, waiting for transfers between devices  101 us
    psum x2, blocking collectives, shards(): block_table = lax.psum(lax.psum(block_table, 'row'), 'col')  43.7 us
    all_gather x1, blocking collectives, shards(): lax.all_gather(rotation, ('row', 'col'), axis=1, tiled=True)  42.3 us
    all_gather x1, blocking collectives, shards(): lax.all_gather(translation, ('row', 'col'), axis=1, tiled=True)  37 us
    dot_general x1, matrix products, edge_terms(): jnp.einsum('aep,bep->eab', scaled_v, jac_v, precision=PRECISE)  18.1 us
    dot_general x1, matrix products, edge_terms(): jnp.einsum('aep,bep->eab', scaled_u, jac_u, precision=PRECISE)  16.7 us
    all_gather x1, waiting for transfers between devices, spread(): return lax.all_gather(nearby, 'col', axis=1, tiled=True)  15.1 us
    dot_general x1, matrix products, shards(): jnp.einsum('aep,bep->eab', coupling * at_edges[:, 0][None], coupling, pre...  14.9 us
  transfers between devices with their start and end apart: 11, of which 9 were waited for; matrix products, arithmetic and copies ran while one was open for 5% of the time, Pallas kernels for 0%

profile of v1, /device:TPU:0, one launch (start us, length us, event | category | flops | bytes accessed | tf_op | source)
XLA Modules:
  0.0 454.0 jit_solution(17753499618536430349)
XLA Ops:
  8.0 5.1 %collective-permute-start.1 = (f32[1,2,3072]{2,0,1:T(1,128)S(1)}, f32[1,2,3072]{2,0,1:T(1,128)S(1)}, u32[]{:S(2)}, u32[]{:S(2)}) collective-permute-start(f32[1,2,3072]{2,0,1:T(1,128)S(1)} %broadcast_in_dim.30), channel_id=1, source_target_pairs={{8,0},{16,8},{24,16},{0,24},{9,1},{17,9},{25,17},{1,25},{10,2},{18... | collective-permute-start | bytes 73736 | tf_op jit(solution)/shard_map/ppermute | solution.py:23
  17.0 42.3 %all-gather = f32[32,2,3]{2,1,0:T(2,128)S(1)} all-gather(f32[1,2,3]{2,1,0:T(2,128)} %bitcast.512), channel_id=1, replica_groups=mesh['row'=4,'col'=8] {'row','col'}, dimensions={0}, use_global_device_ids=true | all-gather | bytes 792 | tf_op jit(solution)/shard_map/all_gather | solution.py:148
  59.4 37.0 %all-gather.1 = f32[32,2,3]{2,1,0:T(2,128)S(1)} all-gather(f32[1,2,3]{2,1,0:T(2,128)} %bitcast.513), channel_id=1, replica_groups=mesh['row'=4,'col'=8] {'row','col'}, dimensions={0}, use_global_device_ids=true | all-gather | bytes 792 | tf_op jit(solution)/shard_map/all_gather | solution.py:149
  97.3 1.8 fusion.181
  101.1 10.5 %all_gather.14 = f32[3,16,3072]{2,0,1:T(4,128)S(1)} all-gather(f32[3,2,3072]{2,0,1:T(4,128)S(1)} %pad_maximum_fusion.1), channel_id=1, replica_groups=mesh['row'=4,'col'=8] {'col'}, dimensions={1}, use_global_device_ids=true | all-gather | bytes 663552 | tf_op jit(solution)/shard_map/all_gather | solution.py:122
  112.9 2.0 multiply_dynamic-update-slice_fusion.3
  114.9 1.5 fusion.32
  116.6 1.8 fusion.17
  118.5 1.2 multiply_dynamic-update-slice_fusion.2
  119.7 1.1 multiply_dynamic-update-slice_fusion.1
  121.7 1.1 constant_dynamic-update-slice_fusion.1
  122.8 1.4 multiply_dynamic-update-slice_fusion
  124.2 48.7 %all-reduce.5.cloned.1.call-done = f32[3,16,2,3072]{3,1,2,0:T(8,128)} async-done(((f32[3,16,2,3072]{3,1,2,0:T(8,128)}), f32[3,16,2,3072]{3,1,2,0:T(8,128)}) %all-reduce.5.cloned.1.call-update) | async-done | bytes 1179664
  173.0 1.1 dynamic-slice_bitcast_fusion.1
  174.0 3.3 collective-permute-start.2
  177.4 1.2 multiply_dynamic-update-slice_fusion.6
  179.1 4.3 collective-permute-done.3
  184.6 2.0 collective-permute-start.4
  186.6 1.1 multiply_dynamic-update-slice_fusion.5
  187.7 1.0 collective-permute-done.5
  188.7 1.9 collective-permute-done.4
  191.9 1.1 constant_dynamic-update-slice_fusion
  193.8 1.2 multiply_dynamic-update-slice_fusion.4
  195.1 1.9 bitcast_subtract_fusion.1
  197.0 15.1 %all-gather.4.cloned.1.call-done = f32[3,16,2,3072]{3,2,0,1:T(2,128)} async-done(((f32[3,2,2,3072]{3,2,0,1:T(2,128)}), f32[3,16,2,3072]{3,2,0,1:T(2,128)}) %all-gather.4.cloned.1.call-update) | async-done | bytes 1179664 | tf_op jit(solution)/shard_map/all_gather | solution.py:122
  212.1 1.7 copy.35
  214.6 1.9 gather_fusion.1
  218.6 9.1 %broadcast_multiply_fusion = (f32[6,48,3072]{2,1,0:T(8,128)}, f32[6,48,3072]{2,1,0:T(8,128)S(1)}, f32[6,48,3072]{2,1,0:T(8,128)}, f32[6,48,3072]{2,1,0:T(8,128)}) fusion(f32[48,3072]{1,0:T(8,128)} %bitcast.500, f32[48,3072]{1,0:T(8,128)} %get-tuple-element.58, f32[48,3072]{1,0:T(8,128)} %get-tuple-element.55, ...), kind=kLoop, calls=%fused_computation.20 | loop fusion | flops 5308416 | bytes 24182784 | tf_op jit(solution)/shard_map/mul | solution.py:183
  227.7 12.9 %fusion.2 = f32[48,1,6]{2,1,0:T(1,128)} fusion(f32[6,48,3072]{2,1,0:T(8,128)S(1)} %get-tuple-element.39, f32[48,2,3072]{2,1,0:T(2,128)S(1)} %broadcast_select_fusion), kind=kOutput, calls=%fused_computation.4 | convolution fusion | flops 10616832 | bytes 4129920 | tf_op jit(solution)/shard_map/aep,ep->ea/dot_general | solution.py:185
  241.4 18.1 %fusion.8 = f32[48,6,6]{2,1,0:T(8,128)} fusion(f32[6,48,3072]{2,1,0:T(8,128)} %get-tuple-element.41, f32[6,48,3072]{2,1,0:T(8,128)} %get-tuple-element.60), kind=kOutput, calls=%fused_computation.10 | convolution fusion | flops 63700992 | bytes 7084800 | tf_op jit(solution)/shard_map/aep,bep->eab/dot_general | solution.py:83
  259.4 12.8 %fusion.6 = f32[48,1,6]{2,1,0:T(1,128)} fusion(f32[6,48,3072]{2,1,0:T(8,128)S(1)} %copy-done.1, f32[48,3072,1]{1,0,2:T(8,128)S(1)} %bitcast.502), kind=kOutput, calls=%fused_computation.8 | convolution fusion | flops 10616832 | bytes 4129920 | tf_op jit(solution)/shard_map/aep,ep->ea/dot_general | solution.py:86
  273.0 16.7 %fusion.19 = f32[48,6,6]{2,1,0:T(8,128)S(1)} fusion(f32[48,6,6]{2,1,0:T(8,128)} %fusion.8, f32[6,48,3072]{2,1,0:T(8,128)} %multiply_dynamic-update-slice_fusion.4, f32[6,48,3072]{2,1,0:T(8,128)} %get-tuple-element.40), kind=kOutput, calls=%fused_computation.28 | convolution fusion | flops 63702720 | bytes 7091712 | tf_op jit(solution)/shard_map/aep,bep->eab/dot_general | solution.py:83
  289.7 12.9 %fusion.10 = f32[48,1,6]{2,1,0:T(1,128)} fusion(f32[6,48,3072]{2,1,0:T(8,128)S(1)} %copy-done, f32[48,3072,1]{1,0,2:T(8,128)S(1)} %bitcast.501), kind=kOutput, calls=%fused_computation.12 | convolution fusion | flops 10616832 | bytes 4129920 | tf_op jit(solution)/shard_map/aep,ep->ea/dot_general | solution.py:86
  302.7 14.9 %fusion.24 = f32[48,6,6]{2,1,0:T(8,128)} fusion(f32[48,6,6]{2,1,0:T(8,128)S(1)} %fusion.19, f32[6,48,3072]{2,1,0:T(8,128)S(1)} %get-tuple-element.39, f32[6,48,3072]{2,1,0:T(8,128)S(1)} %copy-done.2), kind=kOutput, calls=%fused_computation.29 | convolution fusion | flops 63702720 | bytes 7091712 | tf_op jit(solution)/shard_map/aep,bep->eab/dot_general | solution.py:182
  317.6 1.6 reshape.5281
  320.0 1.4 copy.50
  322.4 1.6 convolution_add_fusion
  324.0 20.2 %psum.14 = f32[64,42]{0,1:T(8,128)} all-reduce(f32[64,42]{0,1:T(8,128)} %convolution_add_fusion), channel_id=1, replica_groups=mesh['row'=4,'col'=8] {'row'}, use_global_device_ids=true, to_apply=%region_1.2 | all-reduce | flops 2688 | bytes 21504 | tf_op jit(solution)/shard_map/psum | solution.py:192
  344.1 23.5 %psum.15 = f32[64,42]{0,1:T(8,128)} all-reduce(f32[64,42]{0,1:T(8,128)} %psum.14), channel_id=1, replica_groups=mesh['row'=4,'col'=8] {'col'}, use_global_device_ids=true, to_apply=%region_2.3 | all-reduce | flops 2688 | bytes 21504 | tf_op jit(solution)/shard_map/psum | solution.py:192
  368.4 1.3 slice.209
  369.7 1.3 reshape.5249
  372.9 1.4 subtract_divide_fusion
  375.9 6.0 %fusion = f32[48,1,3072]{2,1,0:T(1,128)S(1)} fusion(f32[48,6,1]{1,2,0:T(1,128)S(1)} %bitcast.509, f32[6,48,3072]{2,1,0:T(8,128)S(1)} %get-tuple-element.39), kind=kOutput, calls=%fused_computation.2 | convolution fusion | flops 10616832 | bytes 4129920 | tf_op jit(solution)/shard_map/aep,ea->ep/dot_general | solution.py:196
  382.0 1.3 fusion.29
  383.4 52.5 %all-reduce.7.cloned.1.call-done = f32[3,16,3072]{2,1,0:T(8,128)} async-done(((f32[3,16,3072]{2,1,0:T(8,128)}), f32[3,16,3072]{2,1,0:T(8,128)}) %all-reduce.7.cloned.1.call-update) | async-done | bytes 589840
  436.8 3.3 collective-permute-start.6
  441.6 4.1 collective-permute-done.7
  445.7 1.5 fusion.45
  (102 shorter events, 26.0 us)
Async XLA Ops:
  7.2 92.5 %copy-start.21 = (u32[32]{0:T(128)S(1)}, u32[32]{0:T(128)}, u32[]{:S(2)}) copy-start(u32[32]{0:T(128)} %constant.161) | copy-start | bytes 388
  7.2 165.8 %all-reduce.5.cloned.1.call-start = ((), (), s32[]{:S(2)}) async-start(), calls=%async_computation.1 | async-start | bytes 2359296
  8.0 93.1 %collective-permute-start.1 = (f32[1,2,3072]{2,0,1:T(1,128)S(1)}, f32[1,2,3072]{2,0,1:T(1,128)S(1)}, u32[]{:S(2)}, u32[]{:S(2)}) collective-permute-start(f32[1,2,3072]{2,0,1:T(1,128)S(1)} %broadcast_in_dim.30), channel_id=1, source_target_pairs={{8,0},{16,8},{24,16},{0,24},{9,1},{17,9},{25,17},{1,25},{10,2},{18... | collective-permute-start | bytes 73736 | tf_op jit(solution)/shard_map/ppermute | solution.py:23
  13.1 87.9 %collective-permute-start = (f32[1,2,3072]{2,0,1:T(1,128)S(1)}, f32[1,2,3072]{2,0,1:T(1,128)S(1)}, u32[]{:S(2)}, u32[]{:S(2)}) collective-permute-start(f32[1,2,3072]{2,0,1:T(1,128)S(1)} %broadcast_in_dim.30), channel_id=1, source_target_pairs={{0,8},{8,16},{16,24},{24,0},{1,9},{9,17},{17,25},{25,1},{2,10},{10... | collective-permute-start | bytes 73736 | tf_op jit(solution)/shard_map/ppermute | solution.py:21
  13.9 98.1 %copy-start.20 = (s32[48]{0:T(128)}, s32[48]{0:T(128)S(1)}, u32[]{:S(2)}) copy-start(s32[48]{0:T(128)S(1)} %reshape.5243) | copy-start | bytes 580
  15.9 96.2 %copy-start.22 = (s32[48]{0:T(128)}, s32[48]{0:T(128)S(1)}, u32[]{:S(2)}) copy-start(s32[48]{0:T(128)S(1)} %fusion.82) | copy-start | bytes 580
  99.0 15.9 %copy-start.3 = (f32[1,2,24,3072]{3,2,1,0:T(8,128)}, f32[1,2,24,3072]{3,2,1,0:T(8,128)S(1)}, u32[]{:S(2)}) copy-start(f32[1,2,24,3072]{3,2,1,0:T(8,128)S(1)} %get-tuple-element.72) | copy-start | bytes 1769476
  99.0 15.9 %copy-start.4 = (f32[1,2,24,3072]{3,2,1,0:T(8,128)}, f32[1,2,24,3072]{3,2,1,0:T(8,128)S(1)}, u32[]{:S(2)}) copy-start(f32[1,2,24,3072]{3,2,1,0:T(8,128)S(1)} %get-tuple-element.73) | copy-start | bytes 1769476
  112.9 3.6 copy-start.17
  112.9 3.6 copy-start.18
  116.5 2.0 copy-start.7
  116.5 2.0 copy-start.10
  116.5 2.0 copy-start.11
  116.5 2.0 copy-start.12
  116.5 2.0 copy-start.14
  116.5 2.0 copy-start.15
  116.5 6.2 %copy-start.16 = (f32[48]{0:T(128)S(1)}, f32[48]{0:T(128)}, u32[]{:S(2)}) copy-start(f32[48]{0:T(128)} %get-tuple-element.67) | copy-start | bytes 580
  118.4 93.7 %all-gather.4.cloned.1.call-start = ((), (), s32[]{:S(2)}) async-start(), calls=%async_computation | async-start | bytes 1327104 | tf_op jit(solution)/shard_map/all_gather | solution.py:122
  119.7 66.9 %copy-start.13 = (f32[3072]{0:T(1024)S(1)}, f32[3072]{0:T(1024)}, u32[]{:S(2)}) copy-start(f32[3072]{0:T(1024)} %fusion.76) | copy-start | bytes 36868
  174.0 5.1 %collective-permute-start.2 = (f32[2,2,3072]{2,0,1:T(2,128)S(1)}, f32[2,2,3072]{2,0,1:T(2,128)S(1)}, u32[]{:S(2)}, u32[]{:S(2)}) collective-permute-start(f32[2,2,3072]{2,0,1:T(2,128)S(1)} %get-tuple-element.48), channel_id=1, source_target_pairs={{0,24},{8,0},{16,8},{24,16},{1,25},{9,1},{17,9},{25,17},{2,26},{10... | collective-permute-start | bytes 147464 | tf_op jit(solution)/shard_map/ppermute | solution.py:32
  177.4 6.1 %collective-permute-start.3 = (f32[2,2,3072]{2,0,1:T(2,128)S(1)}, f32[2,2,3072]{2,0,1:T(2,128)S(1)}, u32[]{:S(2)}, u32[]{:S(2)}) collective-permute-start(f32[2,2,3072]{2,0,1:T(2,128)S(1)} %get-tuple-element.49), channel_id=1, source_target_pairs={{0,8},{8,16},{16,24},{24,0},{1,9},{9,17},{17,25},{25,1},{2,10},{10... | collective-permute-start | bytes 147464 | tf_op jit(solution)/shard_map/ppermute | solution.py:32
  184.5 4.2 copy-start.8
  184.5 4.2 copy-start.9
  184.5 4.1 collective-permute-start.5
  184.6 5.9 %collective-permute-start.4 = (f32[1,2,2,3072]{3,1,2,0:T(2,128)S(1)}, f32[1,2,2,3072]{3,1,2,0:T(2,128)S(1)}, u32[]{:S(2)}, u32[]{:S(2)}) collective-permute-start(f32[1,2,2,3072]{3,1,2,0:T(2,128)S(1)} %maximum_bitcast_fusion.1), channel_id=1, source_target_pairs={{0,8},{8,16},{16,24},{24,0},{1,9},{9,17},{17,25},{25,1},{2,10},{10... | collective-permute-start | bytes 147464 | tf_op jit(solution)/shard_map/ppermute | solution.py:21
  191.4 244.5 %all-reduce.7.cloned.1.call-start = ((), (), s32[]{:S(2)}) async-start(), calls=%async_computation.2 | async-start | bytes 1179648
  241.4 18.1 %copy-start.1 = (f32[6,48,3072]{2,1,0:T(8,128)S(1)}, f32[6,48,3072]{2,1,0:T(8,128)}, u32[]{:S(2)}) copy-start(f32[6,48,3072]{2,1,0:T(8,128)} %get-tuple-element.41) | copy-start | bytes 10616836
  241.4 18.1 %copy-start.6 = (f32[48,3072]{1,0:T(8,128)S(1)}, f32[48,3072]{1,0:T(8,128)}, u32[]{:S(2)}) copy-start(f32[48,3072]{1,0:T(8,128)} %get-tuple-element.59) | copy-start | bytes 1769476
  273.0 16.7 %copy-start = (f32[6,48,3072]{2,1,0:T(8,128)S(1)}, f32[6,48,3072]{2,1,0:T(8,128)}, u32[]{:S(2)}) copy-start(f32[6,48,3072]{2,1,0:T(8,128)} %get-tuple-element.40) | copy-start | bytes 10616836
  273.0 16.7 %copy-start.5 = (f32[48,3072]{1,0:T(8,128)S(1)}, f32[48,3072]{1,0:T(8,128)}, u32[]{:S(2)}) copy-start(f32[48,3072]{1,0:T(8,128)} %get-tuple-element.54) | copy-start | bytes 1769476
  289.7 13.0 %copy-start.2 = (f32[6,48,3072]{2,1,0:T(8,128)S(1)}, f32[6,48,3072]{2,1,0:T(8,128)}, u32[]{:S(2)}) copy-start(f32[6,48,3072]{2,1,0:T(8,128)} %get-tuple-element.38) | copy-start | bytes 10616836
  317.6 64.4 %copy-start.19 = (s32[48]{0:T(128)S(1)}, s32[48]{0:T(128)}, u32[]{:S(2)}) copy-start(s32[48]{0:T(128)} %get-tuple-element.45) | copy-start | bytes 580
  436.8 4.8 %collective-permute-start.6 = (f32[2,3072]{1,0:T(2,128)S(1)}, f32[2,3072]{1,0:T(2,128)S(1)}, u32[]{:S(2)}, u32[]{:S(2)}) collective-permute-start(f32[2,3072]{1,0:T(2,128)S(1)} %get-tuple-element.62), channel_id=1, source_target_pairs={{0,24},{8,0},{16,8},{24,16},{1,25},{9,1},{17,9},{25,17},{2,26},{10... | collective-permute-start | bytes 73736 | tf_op jit(solution)/shard_map/ppermute | solution.py:32
  440.1 5.6 %collective-permute-start.7 = (f32[2,3072]{1,0:T(2,128)S(1)}, f32[2,3072]{1,0:T(2,128)S(1)}, u32[]{:S(2)}, u32[]{:S(2)}) collective-permute-start(f32[2,3072]{1,0:T(2,128)S(1)} %get-tuple-element.63), channel_id=1, source_target_pairs={{0,8},{8,16},{16,24},{24,0},{1,9},{9,17},{17,25},{25,1},{2,10},{10... | collective-permute-start | bytes 73736 | tf_op jit(solution)/shard_map/ppermute | solution.py:32
Sparse Core Ops, SparseCore 0:
  118.5 54.4 all-reduce.4
  191.5 20.5 all-gather.3
  383.5 52.3 all-reduce.6
